TPU v7x, 512 devices: a whole 4x8x8 slice. The times are simulated.
512 devices in a mesh: seq: 32 (over y, x), head: 16 (over z, core).
Axes of the slice: x: 4, y: 8, z: 8, core: 2. Of those that a mesh axis runs over, the one named last changes fastest.
Arguments:
- x_input: bfloat16 [4096, 16384], P('seq', 'head'), may hold values from -6 to 6
- z_input: bfloat16 [4096, 16384], P('seq', 'head'), may hold values from -52 to 52
- bc_input: bfloat16 [2, 4096, 128], P(None, 'seq'), may hold values from -2.09375 to 2.09375
- dt_raw: float32 [128, 4096], P('head', 'seq'), may hold values from -1.5 to 4.5
- dt_bias: float32 [128], P('head'), may hold values from -4.2 to 0.3
- a_log: float32 [128], P('head')
- d_skip: float32 [128], P('head'), may hold values from 0.5 to 1.5
- conv_x: float32 [4, 16384], P(None, 'head'), may hold values from -3 to 3
- convolution_bc_taps: float32 [2, 4, 128], replicated, may hold values from -3 to 3
- rescale_factor: float32 [16384], P('head'), may hold values from 0.5 to 1.5
- grad_out: bfloat16 [4096, 16384], P('seq', 'head'), may hold values from -40 to 40
Outputs:
- grad_x: bfloat16 [4096, 16384], P('seq', 'head')
- grad_z: bfloat16 [4096, 16384], P('seq', 'head')
- grad_bc: bfloat16 [2, 4096, 128], P(None, ('seq', 'head'))
- grad_dt: float32 [128, 4096], P('head', 'seq')
All inputs are finite; a program needn't handle non-finite values.
Results may differ from a plain program's by a relative error of at most 0.0086.
Values may be sent and summed in bfloat16 or wider, within the bound.
A program may use at most 64 MiB of HBM per device.

v0:
```python
import jax
import jax.numpy as jnp
from jax import lax
from jax.sharding import PartitionSpec as P

INNER = 16384
EPS = 1e-05


def entering(part, axis, combine, identity, reverse):
    count = lax.axis_size(axis)
    place = lax.axis_index(axis)
    ahead = count - 1 - place if reverse else place
    gathered = jax.tree.map(lambda a: lax.all_gather(a, axis), part)
    state = jax.tree.map(lambda a, e: jnp.zeros_like(a) + jnp.asarray(e, a.dtype), part, identity)

    def one(hop, state):
        source = count - 1 - hop if reverse else hop
        return combine(
            state, jax.tree.map(lambda a: lax.dynamic_index_in_dim(a, source, 0, False), gathered)
        )

    return lax.fori_loop(0, ahead, one, state)


def passed_along(block, axis, distance):
    devices = range(lax.axis_size(axis))
    route = [(i - distance, i) for i in devices if i - distance in devices]
    return lax.ppermute(block, axis, route)


def silu_grad(value):
    sigma = jax.nn.sigmoid(value)
    return sigma * (1.0 + value * (1.0 - sigma))


def conv_rows(extended, weight_matrix):
    length = extended.shape[-2] - 3
    summed = weight_matrix[..., 0, :][..., None, :] * extended[..., 0:length, :]
    for offset in range(1, 4):
        summed = (
            summed
            + weight_matrix[..., offset, :][..., None, :]
            * extended[..., offset : offset + length, :]
        )
    return summed


def conv_back(extended, weight_matrix):
    length = extended.shape[-2] - 3
    summed = weight_matrix[..., 0, :][..., None, :] * extended[..., 3 : 3 + length, :]
    for offset in range(1, 4):
        summed = (
            summed
            + weight_matrix[..., offset, :][..., None, :]
            * extended[..., 3 - offset : 3 - offset + length, :]
        )
    return summed


def decay_of(cumul, causal):
    between = cumul[:, None] - cumul[None, :]
    return jnp.where(causal, jnp.exp(jnp.minimum(between, 0.0)), 0.0)


def weighted_rows(trailing_decay, step_size, b_rows):
    return ((trailing_decay * step_size)[:, None] * b_rows.astype(jnp.float32)).astype(jnp.bfloat16)


def head_forward(cumul, step_size, gram_matrix, x_head, state_low, c_rows, skip_gain, causal):
    decay_matrix = decay_of(cumul, causal)
    mixer_low = (gram_matrix * decay_matrix * step_size[None, :]).astype(jnp.bfloat16)
    intra_out = jnp.dot(mixer_low, x_head, preferred_element_type=jnp.float32)
    handed_forward = jnp.dot(c_rows, state_low, preferred_element_type=jnp.float32)
    return (
        intra_out
        + jnp.exp(cumul)[:, None] * handed_forward
        + skip_gain * x_head.astype(jnp.float32)
    )


def head_backward(
    cumul,
    step_size,
    gram_matrix,
    x_head,
    grad_head,
    state_low,
    state_exact,
    out_low,
    out_exact,
    b_rows,
    c_rows,
    skip_gain,
    decay_rate,
    causal,
):
    decay_matrix = decay_of(cumul, causal)
    mixer_low = (gram_matrix * decay_matrix * step_size[None, :]).astype(jnp.bfloat16)
    grad_mix = jnp.dot(grad_head, x_head.T, preferred_element_type=jnp.float32)
    decayed_grad = grad_mix * decay_matrix
    weighted_grad = decayed_grad * step_size[None, :]
    gram_grad = weighted_grad * gram_matrix
    lifted = jnp.exp(cumul)
    handed_forward = jnp.dot(c_rows, state_low, preferred_element_type=jnp.float32)
    reached = jnp.dot(x_head, out_low.T, preferred_element_type=jnp.float32)
    trailing_decay = jnp.exp(cumul[-1] - cumul)
    inner_b = jnp.sum(b_rows.astype(jnp.float32) * reached, axis=1)
    state_term = trailing_decay * step_size * inner_b
    grad_cumul = jnp.sum(gram_grad, axis=1) - jnp.sum(gram_grad, axis=0)
    grad_cumul = (
        grad_cumul
        + lifted * jnp.sum(grad_head.astype(jnp.float32) * handed_forward, axis=1)
        - state_term
    )
    end_grad = jnp.sum(state_term) + jnp.exp(cumul[-1]) * jnp.sum(out_exact * state_exact)
    grad_cumul = grad_cumul.at[-1].add(end_grad)
    grad_log = jnp.cumsum(grad_cumul[::-1])[::-1]
    grad_step = (
        jnp.sum(decayed_grad * gram_matrix, axis=0)
        + trailing_decay * inner_b
        + decay_rate * grad_log
    )
    weighted_b = weighted_rows(trailing_decay, step_size, b_rows)
    grad_x = jnp.dot(mixer_low.T, grad_head, preferred_element_type=jnp.float32)
    grad_x = (
        grad_x
        + skip_gain * grad_head.astype(jnp.float32)
        + jnp.dot(weighted_b, out_low, preferred_element_type=jnp.float32)
    )
    grad_c = lifted[:, None] * jnp.dot(grad_head, state_low.T, preferred_element_type=jnp.float32)
    grad_b = (trailing_decay * step_size)[:, None] * reached
    return (grad_x, grad_step, grad_c, grad_b, weighted_grad)


def block_prep(x_rows, b_rows, step_size, decay_rate):
    length = x_rows.shape[0]
    head_count = step_size.shape[0]
    cumul = jnp.cumsum(decay_rate[:, None] * step_size, axis=1)
    trailing_decay = jnp.exp(cumul[:, -1:] - cumul)
    x_heads = jnp.moveaxis(x_rows.reshape(length, head_count, -1), 1, 0)

    def one_head(head_items):
        weighted_b = weighted_rows(head_items[0], head_items[1], b_rows)
        return jnp.dot(weighted_b.T, head_items[2], preferred_element_type=jnp.float32)

    local_state = lax.map(one_head, (trailing_decay, step_size, x_heads))
    return (cumul, x_heads, local_state)


def block_mix(cumul, step_size, gram_matrix, x_heads, state_low, c_rows, skip_gain, causal):

    def one_head(head_items):
        return head_forward(
            head_items[0],
            head_items[1],
            gram_matrix,
            head_items[2],
            head_items[3],
            c_rows,
            head_items[4],
            causal,
        )

    outputs = lax.map(one_head, (cumul, step_size, x_heads, state_low, skip_gain))
    return jnp.moveaxis(outputs, 0, 1).reshape(outputs.shape[1], -1)


def carry_grad(cumul, c_rows, grad_heads):

    def one_head(head_items):
        lifted_c = (jnp.exp(head_items[0])[:, None] * c_rows.astype(jnp.float32)).astype(
            jnp.bfloat16
        )
        return jnp.dot(lifted_c.T, head_items[1], preferred_element_type=jnp.float32)

    return lax.map(one_head, (cumul, grad_heads))


def block_back(
    cumul,
    step_size,
    gram_matrix,
    x_heads,
    grad_heads,
    state_exact,
    out_exact,
    b_rows,
    c_rows,
    skip_gain,
    decay_rate,
    causal,
):
    length = b_rows.shape[0]
    nstate = b_rows.shape[1]
    state_low = state_exact.astype(jnp.bfloat16)
    out_low = out_exact.astype(jnp.bfloat16)

    def one_head(running, head_items):
        (
            cumulative_head,
            step_head,
            x_head,
            grad_head,
            low_in,
            exact_in,
            low_out,
            exact_out,
            skip_head,
            rate_head,
        ) = head_items
        grad_x, grad_step, grad_c, grad_b, weighted_grad = head_backward(
            cumulative_head,
            step_head,
            gram_matrix,
            x_head,
            grad_head,
            low_in,
            exact_in,
            low_out,
            exact_out,
            b_rows,
            c_rows,
            skip_head,
            rate_head,
            causal,
        )
        return (
            (running[0] + weighted_grad, running[1] + grad_c, running[2] + grad_b),
            (grad_x, grad_step),
        )

    initial = (
        jnp.zeros((length, length), jnp.float32),
        jnp.zeros((length, nstate), jnp.float32),
        jnp.zeros((length, nstate), jnp.float32),
    )
    (grad_sum, c_sum, b_sum), (grad_xs, grad_steps) = lax.scan(
        one_head,
        initial,
        (
            cumul,
            step_size,
            x_heads,
            grad_heads,
            state_low,
            state_exact,
            out_low,
            out_exact,
            skip_gain,
            decay_rate,
        ),
    )
    grad_c = c_sum + jnp.dot(grad_sum, b_rows.astype(jnp.float32), precision=lax.Precision.HIGHEST)
    grad_b = b_sum + jnp.dot(
        grad_sum.T, c_rows.astype(jnp.float32), precision=lax.Precision.HIGHEST
    )
    grad_x = jnp.moveaxis(grad_xs, 0, 1).reshape(length, -1)
    return (grad_x, jnp.stack([grad_b, grad_c]), grad_steps)


def pass_states(totals, states, reverse):
    factor = jnp.exp(totals)[:, None, None]

    def combine(earlier, latter):
        return (earlier[0] * latter[0], latter[0] * earlier[1] + latter[1])

    result = entering(
        (factor, states), "seq", combine, (jnp.ones_like(factor), jnp.zeros_like(states)), reverse
    )
    return result[1]


def shards(
    x_input,
    z_input,
    bc_input,
    dt_raw,
    dt_bias,
    a_log,
    d_skip,
    conv_x,
    convolution_bc_taps,
    rescale_factor,
    grad_out,
):
    length = x_input.shape[0]
    head_count = dt_raw.shape[0]
    decay_rate = -jnp.exp(a_log)
    step_size = jax.nn.softplus(dt_raw + dt_bias[:, None])
    causal = jnp.tril(jnp.ones((length, length), dtype=bool))
    rows_prior = passed_along((x_input[length - 3 :], bc_input[:, length - 3 :]), "seq", 1)
    x_ext = jnp.concatenate([rows_prior[0], x_input], axis=0)
    bc_ext = jnp.concatenate([rows_prior[1], bc_input], axis=1)
    x_pre = conv_rows(x_ext.astype(jnp.float32), conv_x)
    bc_pre = conv_rows(bc_ext.astype(jnp.float32), convolution_bc_taps)
    x_rows = jax.nn.silu(x_pre).astype(jnp.bfloat16)
    bc_rows = jax.nn.silu(bc_pre).astype(jnp.bfloat16)
    gram_matrix = jnp.dot(bc_rows[1], bc_rows[0].T, preferred_element_type=jnp.float32)
    cumul, x_heads, local_state = block_prep(x_rows, bc_rows[0], step_size, decay_rate)
    totals = cumul[:, -1]
    state_exact = pass_states(totals, local_state, False)
    mixed_out = block_mix(
        cumul,
        step_size,
        gram_matrix,
        x_heads,
        state_exact.astype(jnp.bfloat16),
        bc_rows[1],
        d_skip,
        causal,
    )
    z_rows = z_input.astype(jnp.float32)
    gate_value = jax.nn.silu(z_rows)
    gated = mixed_out * gate_value
    square_sum = lax.psum(jnp.sum(gated * gated, axis=1), "head")
    inv_rms = lax.rsqrt(square_sum / INNER + EPS)
    normed = gated * inv_rms[:, None]
    scaled = grad_out.astype(jnp.float32) * rescale_factor
    product_sum = lax.psum(jnp.sum(scaled * normed, axis=1), "head")
    mean_dot = product_sum / INNER
    grad_gated = inv_rms[:, None] * (scaled - normed * mean_dot[:, None])
    grad_z = (grad_gated * mixed_out * silu_grad(z_rows)).astype(jnp.bfloat16)
    grad_mixed = (grad_gated * gate_value).astype(jnp.bfloat16)
    grad_heads = jnp.moveaxis(grad_mixed.reshape(length, head_count, -1), 1, 0)
    state_grad = carry_grad(cumul, bc_rows[1], grad_heads)
    out_exact = pass_states(totals, state_grad, True)
    grad_x_rows, grad_bc_rows, grad_steps = block_back(
        cumul,
        step_size,
        gram_matrix,
        x_heads,
        grad_heads,
        state_exact,
        out_exact,
        bc_rows[0],
        bc_rows[1],
        d_skip,
        decay_rate,
        causal,
    )
    grad_x_pre = grad_x_rows * silu_grad(x_pre)
    row_share = length // lax.axis_size("head")
    first_row = lax.axis_index("head") * row_share
    grad_bc_all = lax.psum(grad_bc_rows, "head")
    grad_bc_pre = grad_bc_all * silu_grad(bc_pre)
    rows_next = passed_along((grad_x_pre[:3], grad_bc_pre[:, :3]), "seq", -1)
    grad_x = conv_back(jnp.concatenate([grad_x_pre, rows_next[0]], axis=0), conv_x).astype(
        jnp.bfloat16
    )
    grad_bc_full = conv_back(
        jnp.concatenate([grad_bc_pre, rows_next[1]], axis=1), convolution_bc_taps
    )
    grad_bc = lax.dynamic_slice_in_dim(grad_bc_full, first_row, row_share, 1).astype(jnp.bfloat16)
    grad_dt = grad_steps * jax.nn.sigmoid(dt_raw + dt_bias[:, None])
    return (grad_x, grad_z, grad_bc, grad_dt)


def solution(mesh):
    return jax.shard_map(
        shards,
        mesh=mesh,
        in_specs=(
            P("seq", "head"),
            P("seq", "head"),
            P(None, "seq", None),
            P("head", "seq"),
            P("head"),
            P("head"),
            P("head"),
            P(None, "head"),
            P(),
            P("head"),
            P("seq", "head"),
        ),
        out_specs=(
            P("seq", "head"),
            P("seq", "head"),
            P(None, ("seq", "head"), None),
            P("head", "seq"),
        ),
        check_vma=False,
    )
```

profile of v0, /device:TPU:30, one launch (start us, length us, event | category | flops | bytes accessed | tf_op | source)
XLA Modules:
  0.0 696.2 jit_solution(10006820068092498792)
XLA Ops:
  8.0 4.6 collective-permute-start
  13.3 3.4 collective-permute-start.1
  23.6 2.3 while.85
  28.9 69.7 %all-reduce = f32[256]{0:T(256)S(1)} all-reduce(f32[256]{0:T(256)S(1)} %dynamic-update-slice.5), channel_id=2, replica_groups=mesh['seq'=32,'head'=16] {'seq'}, use_global_device_ids=true, to_apply=%add | all-reduce | flops 256 | bytes 2048
  98.9 73.7 %all-gather.6.cloned.1.call-done = f32[256,128,128]{2,1,0:T(8,128)} async-done(((f32[8,128,128]{2,1,0:T(8,128)}), f32[256,128,128]{2,1,0:T(8,128)}) %all-gather.6.cloned.1.call-update) | async-done | bytes 16777232 | tf_op jit(solution)/shard_map/all_gather | solution.py:14
  172.6 18.5 %while.86 = (s32[]{:T(128)}, f32[8,128,128]{2,1,0:T(8,128)S(1)}, s32[]{:T(128)}, f32[32,8,1,1]{1,3,2,0:T(1,128)S(1)}, f32[32,8,128,128]{3,2,1,0:T(8,128)}) while((s32[]{:T(128)}, f32[8,128,128]{2,1,0:T(8,128)S(1)}, s32[]{:T(128)}, f32[32,8,1,1]{1,3,2,0:T(1,128)S(1)}, f32[32,8,128,128]{3,2,1,0:T(8,128)}) %tuple.221), condition=%wide.region_4.5_spmd.clone, body=%wide.region_3.4_spmd.sunk.clone | while | flops 262149 | bytes 1573063 | solution.py:23
  191.3 13.1 %while.89 = (s32[]{:T(128)}, f32[8,128,128]{2,1,0:T(8,128)S(1)}, f32[8,128]{1,0:T(8,128)S(1)}, f32[128,128]{1,0:T(8,128)S(1)}, f32[8,128]{1,0:T(8,128)S(1)}, /*i...) while((s32[]{:T(128)}, f32[8,128,128]{2,1,0:T(8,128)S(1)}, ...), condition=%wide.region_6.7_spmd.clone.clone, body=%wide.region_5.6_spmd.clone.sunk.clone | while | flops 8585218 | bytes 399477 | solution.py:165
  204.7 26.9 %psum.21 = f32[128]{0:T(128)S(1)} all-reduce(f32[128]{0:T(128)S(1)} %multiply_reduce_fusion.4), channel_id=1, replica_groups=mesh['seq'=32,'head'=16] {'head'}, use_global_device_ids=true, to_apply=%region_8.9 | all-reduce | flops 128 | bytes 1024 | tf_op jit(solution)/shard_map/psum | solution.py:316
  232.0 23.5 %psum.22 = f32[128]{0:T(128)S(1)} all-reduce(f32[128]{0:T(128)S(1)} %multiply_reduce_fusion.3), channel_id=1, replica_groups=mesh['seq'=32,'head'=16] {'head'}, use_global_device_ids=true, to_apply=%region_10.11 | all-reduce | flops 128 | bytes 1024 | tf_op jit(solution)/shard_map/psum | solution.py:320
  256.7 2.3 while.87
  260.1 157.1 %all-gather.8.cloned.1.call-done = f32[256,128,128]{2,1,0:T(8,128)} async-done(((f32[8,128,128]{2,1,0:T(8,128)}), f32[256,128,128]{2,1,0:T(8,128)}) %all-gather.8.cloned.1.call-update) | async-done | bytes 16777232 | tf_op jit(solution)/shard_map/all_gather | solution.py:14
  417.2 19.7 %while.88 = (s32[]{:T(128)}, f32[8,128,128]{2,1,0:T(8,128)S(1)}, s32[]{:T(128)}, f32[32,8,1,1]{1,3,2,0:T(1,128)S(1)}, f32[32,8,128,128]{3,2,1,0:T(8,128)}) while((s32[]{:T(128)}, f32[8,128,128]{2,1,0:T(8,128)S(1)}, s32[]{:T(128)}, f32[32,8,1,1]{1,3,2,0:T(1,128)S(1)}, f32[32,8,128,128]{3,2,1,0:T(8,128)}) %tuple.222), condition=%wide.region_14.15_spmd.clone, body=%wide.region_13.14_spmd.sunk.clone | while | flops 262150 | bytes 1573075 | solution.py:23
  437.8 112.0 %while.90 = (s32[]{:T(128)}, f32[128,128]{1,0:T(8,128)S(1)}, f32[128,128]{1,0:T(8,128)S(1)}, f32[128,128]{0,1:T(8,128)S(1)}, f32[8,128,128]{2,1,0:T(8,128)S(1)},...) while((s32[]{:T(128)}, f32[128,128]{1,0:T(8,128)S(1)}, ...), condition=%wide.region_24.25_spmd.clone.clone, body=%wide.region_15.24_spmd.clone.sunk.clone | while | flops 25854976 | bytes 1473321 | solution.py:238
  447.1 1.3 dynamic_update_slice.44
  461.1 1.3 dynamic_update_slice.44
  475.1 1.3 dynamic_update_slice.44
  489.1 1.3 dynamic_update_slice.44
  503.1 1.3 dynamic_update_slice.44
  551.2 4.3 collective-permute-start.2
  555.5 1.4 divide_multiply_fusion
  556.9 3.3 collective-permute-done.2
  561.1 118.1 %all-reduce.3.cloned.1.call-done = f32[2,128,128]{2,1,0:T(8,128)} async-done(((f32[2,128,128]{2,1,0:T(8,128)}), f32[2,128,128]{2,1,0:T(8,128)}) %all-reduce.3.cloned.1.call-update) | async-done | bytes 131088 | tf_op jit(solution)/shard_map/psum | solution.py:345
  680.2 2.8 collective-permute-start.3
  683.0 6.0 collective-permute-done.3
  (380 shorter events, 161.4 us)
Async XLA Ops:
  7.2 184.1 %copy-start.7 = (f32[8]{0:T(128)S(1)}, f32[8]{0:T(128)}, u32[]{:S(2)}) copy-start(f32[8]{0:T(128)} %param.31) | copy-start | bytes 100
  7.2 197.3 %copy-start = (bf16[128,1024]{1,0:T(8,128)(2,1)S(1)}, bf16[128,1024]{1,0:T(8,128)(2,1)}, u32[]{:S(2)}) copy-start(bf16[128,1024]{1,0:T(8,128)(2,1)} %param.26) | copy-start | bytes 786436
  7.2 224.5 %copy-start.4 = (f32[1024]{0:T(1024)S(1)}, f32[1024]{0:T(1024)}, u32[]{:S(2)}) copy-start(f32[1024]{0:T(1024)} %param.34) | copy-start | bytes 12292
  7.2 224.5 %copy-start.3 = (bf16[128,1024]{1,0:T(8,128)(2,1)S(1)}, bf16[128,1024]{1,0:T(8,128)(2,1)}, u32[]{:S(2)}) copy-start(bf16[128,1024]{1,0:T(8,128)(2,1)} %param.35) | copy-start | bytes 786436
  7.2 165.4 %all-gather.6.cloned.1.call-start = ((), (), s32[]{:S(2)}) async-start(), calls=%async_computation.1 | async-start | bytes 17301504 | tf_op jit(solution)/shard_map/all_gather | solution.py:14
  8.0 12.5 %collective-permute-start = (bf16[2,3,128]{2,1,0:T(4,128)(2,1)S(1)}, bf16[2,3,128]{2,1,0:T(4,128)(2,1)S(1)}, u32[]{:S(2)}, u32[]{:S(2)}) collective-permute-start(bf16[2,3,128]{2,1,0:T(4,128)(2,1)S(1)} %slice.125), channel_id=1, source_target_pairs={{0,16},{16,32},{32,48},{48,64},{64,80},{80,96},{96,112},{112,128},... | collective-permute-start | bytes 4616 | tf_op jit(solution)/shard_map/ppermute | solution.py:29
  13.3 8.7 %collective-permute-start.1 = (bf16[3,1024]{1,0:T(4,128)(2,1)S(1)}, bf16[3,1024]{1,0:T(4,128)(2,1)S(1)}, u32[]{:S(2)}, u32[]{:S(2)}) collective-permute-start(bf16[3,1024]{1,0:T(4,128)(2,1)S(1)} %slice.135), channel_id=1, source_target_pairs={{0,16},{16,32},{32,48},{48,64},{64,80},{80,96},{96,112},{112,128},... | collective-permute-start | bytes 18440 | tf_op jit(solution)/shard_map/ppermute | solution.py:29
  18.3 0.8 copy-start.6
  25.9 0.8 copy-start.1
  26.7 390.5 %all-gather.8.cloned.1.call-start = ((), (), s32[]{:S(2)}) async-start(), calls=%async_computation.2 | async-start | bytes 17301504 | tf_op jit(solution)/shard_map/all_gather | solution.py:14
  191.2 364.3 %copy-start.5 = (f32[8,128]{1,0:T(8,128)S(1)}, f32[8,128]{1,0:T(8,128)}, u32[]{:S(2)}) copy-start(f32[8,128]{1,0:T(8,128)} %param.28) | copy-start | bytes 12292
  259.0 0.8 copy-start.2
  259.9 419.3 %all-reduce.3.cloned.1.call-start = ((), (), s32[]{:S(2)}) async-start(), calls=%async_computation | async-start | bytes 262144 | tf_op jit(solution)/shard_map/psum | solution.py:345
  551.2 9.0 %collective-permute-start.2 = (f32[3,1024]{1,0:T(4,128)S(1)}, f32[3,1024]{1,0:T(4,128)S(1)}, u32[]{:S(2)}, u32[]{:S(2)}) collective-permute-start(f32[3,1024]{1,0:T(4,128)S(1)} %slice.164), channel_id=1, source_target_pairs={{16,0},{32,16},{48,32},{64,48},{80,64},{96,80},{112,96},{128,112},... | collective-permute-start | bytes 36872 | tf_op jit(solution)/shard_map/ppermute | solution.py:29
  680.2 8.8 %collective-permute-start.3 = (f32[2,3,128]{2,1,0:T(4,128)S(1)}, f32[2,3,128]{2,1,0:T(4,128)S(1)}, u32[]{:S(2)}, u32[]{:S(2)}) collective-permute-start(f32[2,3,128]{2,1,0:T(4,128)S(1)} %slice.169), channel_id=1, source_target_pairs={{16,0},{32,16},{48,32},{64,48},{80,64},{96,80},{112,96},{128,112},... | collective-permute-start | bytes 9224 | tf_op jit(solution)/shard_map/ppermute | solution.py:29
Sparse Core Ops, SparseCore 0:
  26.8 145.7 all-gather.5
  260.0 157.1 all-gather.7
  551.1 128.0 all-reduce.2
where the time goes:
time: 700 us; the launch traced here: 696 us
  waiting for transfers between devices  358 us (51%)
  blocking collectives  120 us (17%)
  other arithmetic  78.8 us (11%)
  local copies, waits for them, and re-layouts  50.1 us (7%)
  matrix products  40.3 us (6%)
  loops' own time  18.7 us (3%)
  starting transfers between devices  15.2 us (2%)
  between operations  14.8 us (2%)
    all_gather x2, waiting for transfers between devices, entering(): gathered = jax.tree.map(lambda a: lax.all_gather(a, axis), part)  231 us
    psum x1, waiting for transfers between devices, shards(): grad_bc_all = lax.psum(grad_bc_rows, 'head')  118 us
    unnamed x1, blocking collectives  69.7 us
    add x31, other arithmetic, combine(): return (earlier[0] * latter[0], latter[0] * earlier[1] + latter[1])  36.9 us
    psum x1, blocking collectives, shards(): square_sum = lax.psum(jnp.sum(gated * gated, axis=1), 'head')  26.9 us
    dynamic_slice x24, local copies, waits for them, and re-layouts, block_mix(): lax.map(one_head, (cumul, step_size, x_heads, state_low, skip_gain))  24.8 us
    psum x1, blocking collectives, shards(): product_sum = lax.psum(jnp.sum(scaled * normed, axis=1), 'head')  23.5 us
    another operation x1, loops' own time, block_back(): lax.scan(one_head, initial, (cumul, step_size, x_heads, grad_heads, state...  16.9 us
  transfers between devices with their start and end apart: 7, of which 5 were waited for; matrix products, arithmetic and copies ran while one was open for 2% of the time, Pallas kernels for 0%

commit v1 on v0

--- a/solution.py
+++ b/solution.py
@@ -313,7 +313,9 @@
     z_rows = z_input.astype(jnp.float32)
     gate_value = jax.nn.silu(z_rows)
     gated = mixed_out * gate_value
-    square_sum = lax.psum(jnp.sum(gated * gated, axis=1), "head")
+    x = jnp.sum(gated * gated, axis=1)
+    parts = lax.all_gather(x, "head")
+    square_sum = jnp.sum(parts, axis=0)
     inv_rms = lax.rsqrt(square_sum / INNER + EPS)
     normed = gated * inv_rms[:, None]
     scaled = grad_out.astype(jnp.float32) * rescale_factor

time: 700 us -> 693 us (0.990)
  blocking collectives: 120 us -> 112 us
    psum x1 -> x0, blocking collectives: 26.9 us -> none  [shards(): square_sum = lax.psum(jnp.sum(gated * gated, axis=1), 'head')]
    all_gather x0 -> x1, blocking collectives: none -> 18.2 us  [shards(): parts = lax.all_gather(x, 'head')]
where the time goes in v1:
time: 693 us; the launch traced here: 689 us
  waiting for transfers between devices  359 us (52%)
  blocking collectives  112 us (16%)
  other arithmetic  78.8 us (11%)
  local copies, waits for them, and re-layouts  50.1 us (7%)
  matrix products  40.3 us (6%)
  loops' own time  18.7 us (3%)
  starting transfers between devices  15.2 us (2%)
  between operations  14.8 us (2%)
    all_gather x2, waiting for transfers between devices, entering(): gathered = jax.tree.map(lambda a: lax.all_gather(a, axis), part)  232 us
    psum x1, waiting for transfers between devices, shards(): grad_bc_all = lax.psum(grad_bc_rows, 'head')  118 us
    unnamed x1, blocking collectives  69.7 us
    add x31, other arithmetic, combine(): return (earlier[0] * latter[0], latter[0] * earlier[1] + latter[1])  36.9 us
    dynamic_slice x24, local copies, waits for them, and re-layouts, block_mix(): lax.map(one_head, (cumul, step_size, x_heads, state_low, skip_gain))  24.8 us
    psum x1, blocking collectives, shards(): product_sum = lax.psum(jnp.sum(scaled * normed, axis=1), 'head')  23.8 us
    all_gather x1, blocking collectives, shards(): parts = lax.all_gather(x, 'head')  18.2 us
    another operation x1, loops' own time, block_back(): lax.scan(one_head, initial, (cumul, step_size, x_heads, grad_heads, state...  16.9 us
  transfers between devices with their start and end apart: 7, of which 5 were waited for; matrix products, arithmetic and copies ran while one was open for 2% of the time, Pallas kernels for 0%

profile of v1, /device:TPU:30, one launch (start us, length us, event | category | flops | bytes accessed | tf_op | source)
XLA Modules:
  0.0 688.6 jit_solution(7793949799260121262)
XLA Ops:
  8.0 4.6 collective-permute-start
  13.3 3.4 collective-permute-start.1
  23.6 2.3 while.85
  28.9 69.7 %all-reduce = f32[256]{0:T(256)S(1)} all-reduce(f32[256]{0:T(256)S(1)} %dynamic-update-slice.5), channel_id=2, replica_groups=mesh['seq'=32,'head'=16] {'seq'}, use_global_device_ids=true, to_apply=%add | all-reduce | flops 256 | bytes 2048
  98.9 73.7 %all-gather.8.cloned.1.call-done = f32[256,128,128]{2,1,0:T(8,128)} async-done(((f32[8,128,128]{2,1,0:T(8,128)}), f32[256,128,128]{2,1,0:T(8,128)}) %all-gather.8.cloned.1.call-update) | async-done | bytes 16777232 | tf_op jit(solution)/shard_map/all_gather | solution.py:14
  172.6 18.5 %while.86 = (s32[]{:T(128)}, f32[8,128,128]{2,1,0:T(8,128)S(1)}, s32[]{:T(128)}, f32[32,8,1,1]{1,3,2,0:T(1,128)S(1)}, f32[32,8,128,128]{3,2,1,0:T(8,128)}) while((s32[]{:T(128)}, f32[8,128,128]{2,1,0:T(8,128)S(1)}, s32[]{:T(128)}, f32[32,8,1,1]{1,3,2,0:T(1,128)S(1)}, f32[32,8,128,128]{3,2,1,0:T(8,128)}) %tuple.221), condition=%wide.region_4.5_spmd.clone, body=%wide.region_3.4_spmd.sunk.clone | while | flops 262149 | bytes 1573063 | solution.py:23
  191.3 13.1 %while.89 = (s32[]{:T(128)}, f32[8,128,128]{2,1,0:T(8,128)S(1)}, f32[8,128]{1,0:T(8,128)S(1)}, f32[128,128]{1,0:T(8,128)S(1)}, f32[8,128]{1,0:T(8,128)S(1)}, /*i...) while((s32[]{:T(128)}, f32[8,128,128]{2,1,0:T(8,128)S(1)}, ...), condition=%wide.region_6.7_spmd.clone.clone, body=%wide.region_5.6_spmd.clone.sunk.clone | while | flops 8585218 | bytes 399477 | solution.py:165
  204.7 18.2 %all-gather.4 = f32[16,1,128]{2,1,0:T(1,128)S(1)} all-gather(f32[1,1,128]{2,1,0:T(1,128)S(1)} %bitcast.334), channel_id=4, replica_groups=mesh['seq'=32,'head'=16] {'head'}, dimensions={0}, use_global_device_ids=true | all-gather | bytes 8704 | tf_op jit(solution)/shard_map/all_gather | solution.py:317
  223.3 23.8 %psum.14 = f32[128]{0:T(128)S(1)} all-reduce(f32[128]{0:T(128)S(1)} %multiply_reduce_fusion.3), channel_id=1, replica_groups=mesh['seq'=32,'head'=16] {'head'}, use_global_device_ids=true, to_apply=%region_10.11 | all-reduce | flops 128 | bytes 1024 | tf_op jit(solution)/shard_map/psum | solution.py:322
  248.3 2.3 while.87
  251.7 157.9 %all-gather.10.cloned.1.call-done = f32[256,128,128]{2,1,0:T(8,128)} async-done(((f32[8,128,128]{2,1,0:T(8,128)}), f32[256,128,128]{2,1,0:T(8,128)}) %all-gather.10.cloned.1.call-update) | async-done | bytes 16777232 | tf_op jit(solution)/shard_map/all_gather | solution.py:14
  409.6 19.7 %while.88 = (s32[]{:T(128)}, f32[8,128,128]{2,1,0:T(8,128)S(1)}, s32[]{:T(128)}, f32[32,8,1,1]{1,3,2,0:T(1,128)S(1)}, f32[32,8,128,128]{3,2,1,0:T(8,128)}) while((s32[]{:T(128)}, f32[8,128,128]{2,1,0:T(8,128)S(1)}, s32[]{:T(128)}, f32[32,8,1,1]{1,3,2,0:T(1,128)S(1)}, f32[32,8,128,128]{3,2,1,0:T(8,128)}) %tuple.222), condition=%wide.region_14.15_spmd.clone, body=%wide.region_13.14_spmd.sunk.clone | while | flops 262150 | bytes 1573075 | solution.py:23
  430.2 112.0 %while.90 = (s32[]{:T(128)}, f32[128,128]{1,0:T(8,128)S(1)}, f32[128,128]{1,0:T(8,128)S(1)}, f32[128,128]{0,1:T(8,128)S(1)}, f32[8,128,128]{2,1,0:T(8,128)S(1)},...) while((s32[]{:T(128)}, f32[128,128]{1,0:T(8,128)S(1)}, ...), condition=%wide.region_24.25_spmd.clone.clone, body=%wide.region_15.24_spmd.clone.sunk.clone | while | flops 25854976 | bytes 1473321 | solution.py:238
  439.6 1.3 dynamic_update_slice.44
  453.6 1.3 dynamic_update_slice.44
  467.6 1.3 dynamic_update_slice.44
  481.6 1.3 dynamic_update_slice.44
  495.6 1.3 dynamic_update_slice.44
  543.6 4.3 collective-permute-start.2
  547.9 1.4 divide_multiply_fusion
  549.3 3.3 collective-permute-done.2
  553.5 118.1 %all-reduce.3.cloned.1.call-done = f32[2,128,128]{2,1,0:T(8,128)} async-done(((f32[2,128,128]{2,1,0:T(8,128)}), f32[2,128,128]{2,1,0:T(8,128)}) %all-reduce.3.cloned.1.call-update) | async-done | bytes 131088 | tf_op jit(solution)/shard_map/psum | solution.py:347
  672.7 2.8 collective-permute-start.3
  675.4 6.0 collective-permute-done.3
  (381 shorter events, 161.4 us)
Async XLA Ops:
  7.2 184.1 %copy-start.7 = (f32[8]{0:T(128)S(1)}, f32[8]{0:T(128)}, u32[]{:S(2)}) copy-start(f32[8]{0:T(128)} %param.31) | copy-start | bytes 100
  7.2 197.3 %copy-start = (bf16[128,1024]{1,0:T(8,128)(2,1)S(1)}, bf16[128,1024]{1,0:T(8,128)(2,1)}, u32[]{:S(2)}) copy-start(bf16[128,1024]{1,0:T(8,128)(2,1)} %param.26) | copy-start | bytes 786436
  7.2 215.8 %copy-start.4 = (f32[1024]{0:T(1024)S(1)}, f32[1024]{0:T(1024)}, u32[]{:S(2)}) copy-start(f32[1024]{0:T(1024)} %param.34) | copy-start | bytes 12292
  7.2 215.8 %copy-start.3 = (bf16[128,1024]{1,0:T(8,128)(2,1)S(1)}, bf16[128,1024]{1,0:T(8,128)(2,1)}, u32[]{:S(2)}) copy-start(bf16[128,1024]{1,0:T(8,128)(2,1)} %param.35) | copy-start | bytes 786436
  7.2 165.4 %all-gather.8.cloned.1.call-start = ((), (), s32[]{:S(2)}) async-start(), calls=%async_computation.1 | async-start | bytes 17301504 | tf_op jit(solution)/shard_map/all_gather | solution.py:14
  8.0 12.5 %collective-permute-start = (bf16[2,3,128]{2,1,0:T(4,128)(2,1)S(1)}, bf16[2,3,128]{2,1,0:T(4,128)(2,1)S(1)}, u32[]{:S(2)}, u32[]{:S(2)}) collective-permute-start(bf16[2,3,128]{2,1,0:T(4,128)(2,1)S(1)} %slice.125), channel_id=1, source_target_pairs={{0,16},{16,32},{32,48},{48,64},{64,80},{80,96},{96,112},{112,128},... | collective-permute-start | bytes 4616 | tf_op jit(solution)/shard_map/ppermute | solution.py:29
  13.3 8.7 %collective-permute-start.1 = (bf16[3,1024]{1,0:T(4,128)(2,1)S(1)}, bf16[3,1024]{1,0:T(4,128)(2,1)S(1)}, u32[]{:S(2)}, u32[]{:S(2)}) collective-permute-start(bf16[3,1024]{1,0:T(4,128)(2,1)S(1)} %slice.135), channel_id=1, source_target_pairs={{0,16},{16,32},{32,48},{48,64},{64,80},{80,96},{96,112},{112,128},... | collective-permute-start | bytes 18440 | tf_op jit(solution)/shard_map/ppermute | solution.py:29
  18.3 0.8 copy-start.6
  25.9 0.8 copy-start.1
  26.7 382.9 %all-gather.10.cloned.1.call-start = ((), (), s32[]{:S(2)}) async-start(), calls=%async_computation.2 | async-start | bytes 17301504 | tf_op jit(solution)/shard_map/all_gather | solution.py:14
  191.2 356.7 %copy-start.5 = (f32[8,128]{1,0:T(8,128)S(1)}, f32[8,128]{1,0:T(8,128)}, u32[]{:S(2)}) copy-start(f32[8,128]{1,0:T(8,128)} %param.28) | copy-start | bytes 12292
  250.7 0.8 copy-start.2
  251.5 420.1 %all-reduce.3.cloned.1.call-start = ((), (), s32[]{:S(2)}) async-start(), calls=%async_computation | async-start | bytes 262144 | tf_op jit(solution)/shard_map/psum | solution.py:347
  543.6 9.0 %collective-permute-start.2 = (f32[3,1024]{1,0:T(4,128)S(1)}, f32[3,1024]{1,0:T(4,128)S(1)}, u32[]{:S(2)}, u32[]{:S(2)}) collective-permute-start(f32[3,1024]{1,0:T(4,128)S(1)} %slice.164), channel_id=1, source_target_pairs={{16,0},{32,16},{48,32},{64,48},{80,64},{96,80},{112,96},{128,112},... | collective-permute-start | bytes 36872 | tf_op jit(solution)/shard_map/ppermute | solution.py:29
  672.7 8.8 %collective-permute-start.3 = (f32[2,3,128]{2,1,0:T(4,128)S(1)}, f32[2,3,128]{2,1,0:T(4,128)S(1)}, u32[]{:S(2)}, u32[]{:S(2)}) collective-permute-start(f32[2,3,128]{2,1,0:T(4,128)S(1)} %slice.169), channel_id=1, source_target_pairs={{16,0},{32,16},{48,32},{64,48},{80,64},{96,80},{112,96},{128,112},... | collective-permute-start | bytes 9224 | tf_op jit(solution)/shard_map/ppermute | solution.py:29
Sparse Core Ops, SparseCore 0:
  26.8 145.7 all-gather.7
  251.6 157.9 all-gather.9
  543.5 128.0 all-reduce.2
